TPU v7x, 256 devices: a whole 4x4x8 slice. The times are simulated.
256 devices in a mesh: wide: 32 (over z, y), slab: 8 (over x, core).
Axes of the slice: x: 4, y: 4, z: 8, core: 2. Of those that a mesh axis runs over, the one named last changes fastest.
Arguments:
- thermal_state: float32 [32, 128, 32, 1024], P('wide', 'slab'), may hold values from -5 to 5
- thermal_spreading_rate: bfloat16 [32, 128, 32, 1024], P('wide', 'slab'), may hold values from 0.5 to 1.5
- flow_speed_vector: bfloat16 [3, 32, 128, 32, 1024], P(None, 'wide', 'slab'), may hold values from -0.796875 to 0.796875
- interface_guess: float32 [32, 2048], P('wide', 'slab'), may hold values from -4 to 4
- partner_facing_rows: int32 [32, 2048], P('wide', 'slab'), may hold values from 0 to 2047, each once within a row
- mismatch_change_matrix: float32 [32, 2048, 128], P('wide', 'slab'), may hold values from -5 to 5
- output_change_matrix: float32 [32, 2048, 128], P('wide', 'slab'), may hold values from -1.8 to 1.8
Outputs:
- temperature_out: float32 [32, 128, 32, 1024], P('wide', 'slab')
- updated_interface_guess: float32 [32, 2048], P('wide', 'slab')
- unitary_basis_factor: float32 [32, 2048, 128], P('wide', 'slab')
Inputs may be any that keep to these rules, and one draw needn't show every extreme that they name: `partner_facing_rows`: each partition's rows of matching are a permutation of its partner's interface rows.
All inputs are finite; a program needn't handle non-finite values.
Results may differ from a plain program's by a relative error of at most 0.0003.
Values may be sent and summed in bfloat16 or wider, within the bound.
No kernel may reach another device: no remote copies, remote signals or barrier semaphores. Data moves between devices by JAX's collectives and lax.ppermute only.
A program may use at most 64 MiB of HBM per device.

v0:
```python
import math
import jax
import jax.numpy as jnp
from jax import lax
from jax.sharding import PartitionSpec as P

INTERFACE_STRIP = 64
SWEEPS = 4
STEP_SIZE = 0.11


def padded(cells, sides, width):
    for axis, dim in sides:
        count = lax.axis_size(axis)
        ends = count - 1
        head = lax.slice_in_dim(cells, 0, width, axis=dim)
        tail = lax.slice_in_dim(cells, cells.shape[dim] - width, cells.shape[dim], axis=dim)
        cells = jnp.concatenate(
            [
                lax.ppermute(tail, axis, [(i, (i + 1) % count) for i in range(ends)]),
                cells,
                lax.ppermute(head, axis, [((i + 1) % count, i) for i in range(ends)]),
            ],
            axis=dim,
        )
    return cells


def partner(value, axis, stride):
    mask = 2**stride
    pairs = [(source, source ^ mask) for source in range(lax.axis_size(axis))]
    return lax.ppermute(value, axis, pairs)


def gather_sum(value, axes):
    count = lax.axis_size(axes)
    copies = jnp.broadcast_to(value[None], (count, *value.shape))
    return jnp.sum(lax.all_to_all(copies, axes, 0, 0, tiled=True), axis=0)


def sum_everywhere(square):
    rows = square.shape[0] // lax.axis_size("slab")
    blocks = square.reshape(-1, rows, square.shape[1])
    mine = jnp.sum(lax.all_to_all(blocks, "slab", 0, 0, tiled=True), axis=0)
    mine = gather_sum(mine, "wide")
    copies = jnp.broadcast_to(mine[None], blocks.shape)
    return lax.all_to_all(copies, "slab", 0, 0, tiled=True).reshape(square.shape)


def surround_wrapper(block_rows, mirror_layer):
    bottom = jnp.zeros((block_rows.shape[0], 1, block_rows.shape[2]), block_rows.dtype)
    stacked = jnp.concatenate([bottom, block_rows, mirror_layer[:, None, :]], axis=1)
    return jnp.pad(stacked, ((0, 0), (0, 0), (1, 1)))


def march_forward(bordered_array, diffuse_subdomain, subdomain_flow_speed):
    centre = bordered_array[1:-1, 1:-1, 1:-1]
    plus_first = bordered_array[2:, 1:-1, 1:-1]
    minus_first = bordered_array[:-2, 1:-1, 1:-1]
    plus_second = bordered_array[1:-1, 2:, 1:-1]
    minus_second = bordered_array[1:-1, :-2, 1:-1]
    plus_third = bordered_array[1:-1, 1:-1, 2:]
    minus_third = bordered_array[1:-1, 1:-1, :-2]
    spread = (
        plus_first
        + minus_first
        + plus_second
        + minus_second
        + plus_third
        + minus_third
        - 6.0 * centre
    )
    carried = 0.5 * (
        subdomain_flow_speed[0].astype(jnp.float32) * (plus_first - minus_first)
        + subdomain_flow_speed[1].astype(jnp.float32) * (plus_second - minus_second)
        + subdomain_flow_speed[2].astype(jnp.float32) * (plus_third - minus_third)
    )
    return centre + STEP_SIZE * (diffuse_subdomain.astype(jnp.float32) * spread - carried)


def shards(
    thermal_state,
    thermal_spreading_rate,
    flow_speed_vector,
    interface_guess,
    partner_facing_rows,
    mismatch_change_matrix,
    output_change_matrix,
):
    subdomain_thermal_state = thermal_state[0]
    diffuse_subdomain = thermal_spreading_rate[0]
    subdomain_flow_speed = flow_speed_vector[:, 0]
    layer_stack = subdomain_thermal_state.shape[0]
    vertical_extent = subdomain_thermal_state.shape[1]
    rows_dev = interface_guess.shape[1]
    mirror_layer = jnp.repeat(interface_guess[0].reshape(layer_stack, -1), INTERFACE_STRIP, axis=1)
    panel = mismatch_change_matrix[0]
    gram_local = lax.dot_general(
        panel,
        panel,
        (((0,), (0,)), ((), ())),
        precision=lax.Precision.HIGHEST,
        preferred_element_type=jnp.float32,
    )
    ghost_padded = jnp.pad(mirror_layer, ((1, 1), (0, 0)))
    for sweep in range(SWEEPS):
        widened_array = padded(subdomain_thermal_state, (("slab", 0),), 1)
        subdomain_thermal_state = march_forward(
            surround_wrapper(widened_array, ghost_padded), diffuse_subdomain, subdomain_flow_speed
        )
    face_means = jnp.mean(
        subdomain_thermal_state[:, vertical_extent - 1, :].reshape(
            layer_stack, -1, INTERFACE_STRIP
        ),
        axis=2,
    )
    face_means = face_means.reshape(1, rows_dev)
    top_bit = lax.axis_size("wide").bit_length() - 2
    partner_own = partner(face_means, "wide", top_bit)
    partner_all = lax.all_gather(partner_own, "slab", axis=1, tiled=True)
    tilde = jnp.take(partner_all[0], partner_facing_rows[0], axis=0)
    resid = tilde - interface_guess[0]
    proj_local = jnp.dot(
        resid, panel, precision=lax.Precision.HIGHEST, preferred_element_type=jnp.float32
    )
    gram_matrix = sum_everywhere(gram_local)
    projection = gather_sum(proj_local, ("wide", "slab"))
    lower_factor = jnp.linalg.cholesky(gram_matrix)
    half_solve = lax.linalg.triangular_solve(
        lower_factor, projection[:, None], left_side=True, lower=True
    )
    coefficients = -lax.linalg.triangular_solve(
        lower_factor, half_solve, left_side=True, lower=True, transpose_a=True
    )[:, 0]
    update = jnp.dot(
        output_change_matrix[0],
        coefficients,
        precision=lax.Precision.HIGHEST,
        preferred_element_type=jnp.float32,
    )
    updated_interface_guess = tilde + update
    total_rows = rows_dev * lax.axis_size("slab") * lax.axis_size("wide")
    scaled = lax.linalg.triangular_solve(
        lower_factor, panel, left_side=False, lower=True, transpose_a=True
    )
    unitary_basis_factor = math.sqrt(total_rows) * scaled
    return (
        subdomain_thermal_state[None],
        updated_interface_guess[None],
        unitary_basis_factor[None],
    )


def solution(mesh):
    return jax.shard_map(
        shards,
        mesh=mesh,
        in_specs=(
            P("wide", "slab", None, None),
            P("wide", "slab", None, None),
            P(None, "wide", "slab", None, None),
            P("wide", "slab"),
            P("wide", "slab"),
            P("wide", "slab", None),
            P("wide", "slab", None),
        ),
        out_specs=(P("wide", "slab", None, None), P("wide", "slab"), P("wide", "slab", None)),
        check_vma=False,
    )
```

profile of v0, /device:TPU:1, one launch (start us, length us, event | category | flops | bytes accessed | tf_op | source)
XLA Modules:
  0.0 155.6 jit_solution(3249432732262084621)
XLA Ops:
  1.7 5.1 %collective-permute-start = (f32[1,32,1024]{2,1,0:T(8,128)S(1)}, f32[1,32,1024]{2,1,0:T(8,128)S(1)}, u32[]{:S(2)}, u32[]{:S(2)}) collective-permute-start(f32[1,32,1024]{2,1,0:T(8,128)S(1)} %get-tuple-element.22), channel_id=1, source_target_pairs={{1,0},{2,1},{3,2},{4,3},{5,4},{6,5},{7,6},{9,8},{10,9},{11,10},{12... | collective-permute-start | bytes 393224 | tf_op jit(solution)/shard_map/ppermute | solution.py:22
  6.8 1.9 %collective-permute-start.1 = (f32[1,32,1024]{2,1,0:T(8,128)S(1)}, f32[1,32,1024]{2,1,0:T(8,128)S(1)}, u32[]{:S(2)}, u32[]{:S(2)}) collective-permute-start(f32[1,32,1024]{2,1,0:T(8,128)S(1)} %get-tuple-element.21), channel_id=1, source_target_pairs={{0,1},{1,2},{2,3},{3,4},{4,5},{5,6},{6,7},{8,9},{9,10},{10,11},{11... | collective-permute-start | bytes 393224 | tf_op jit(solution)/shard_map/ppermute | solution.py:20
  9.3 1.3 reduce.12
  11.7 2.3 %pad_maximum_fusion.3 = f32[18,34,1024]{2,1,0:T(8,128)S(1)} fusion(f32[18,1,1024]{2,1,0:T(1,128)S(1)} %broadcast_in_dim.48, f32[1,32,1024]{2,1,0:T(8,128)S(1)} %collective-permute-done, f32[16,32,1024]{2,1,0:T(8,128)} %bitcast.102, f32[1,32,1024]{2,1,0:T(8,128)} %copy-done.15, f32[34]{0:T(128)S(1)} %pad.74.clone), kind=kLoop, calls=%fused_computation.4 | loop fusion | flops 2506752 | bytes 4939912 | tf_op jit(solution)/shard_map/concatenate | solution.py:52
  14.6 7.1 %fusion.2 = f32[16,32,1024]{2,1,0:T(8,128)S(1)} fusion(f32[16,32,1024]{2,1,0:T(8,128)} %bitcast.103, f32[18,34,1024]{2,1,0:T(8,128)S(1)} %pad_maximum_fusion.3, f32[1,32,1024]{2,1,0:T(8,128)} %copy-done.14, f32[1,32,1024]{2,1,0:T(8,128)S(1)} %copy-done.16, f32[18,1,1024]{2,1,0:T(1,128)S(1)} %broadcast_in_dim.48, bf16[1,16,32,1024]{3,2,1,0:T(8,128)(2,1)S(1)} %copy-done.8, ...), kind=kLoop, calls=%fused_computation.35 | loop fusion | flops 18874368 | bytes 11231232 | tf_op jit(solution)/shard_map/add | solution.py:78
  21.7 1.3 copy-done.6
  23.7 2.4 %collective-permute-start.2 = (f32[1,32,1024]{2,1,0:T(8,128)}, f32[1,32,1024]{2,1,0:T(8,128)}, u32[]{:S(2)}, u32[]{:S(2)}) collective-permute-start(f32[1,32,1024]{2,1,0:T(8,128)} %get-tuple-element.20), channel_id=1, source_target_pairs={{1,0},{2,1},{3,2},{4,3},{5,4},{6,5},{7,6},{9,8},{10,9},{11,10},{12... | collective-permute-start | bytes 393224 | tf_op jit(solution)/shard_map/ppermute | solution.py:22
  26.1 3.5 %collective-permute-start.3 = (f32[1,32,1024]{2,1,0:T(8,128)}, f32[1,32,1024]{2,1,0:T(8,128)}, u32[]{:S(2)}, u32[]{:S(2)}) collective-permute-start(f32[1,32,1024]{2,1,0:T(8,128)} %get-tuple-element.19), channel_id=1, source_target_pairs={{0,1},{1,2},{2,3},{3,4},{4,5},{5,6},{6,7},{8,9},{9,10},{10,11},{11... | collective-permute-start | bytes 393224 | tf_op jit(solution)/shard_map/ppermute | solution.py:20
  31.9 2.2 %pad_maximum_fusion.2 = f32[18,34,1024]{2,1,0:T(8,128)S(1)} fusion(f32[18,1,1024]{2,1,0:T(1,128)S(1)} %broadcast_in_dim.48, f32[1,32,1024]{2,1,0:T(8,128)} %collective-permute-done.2, f32[16,32,1024]{2,1,0:T(8,128)} %copy-done.6, f32[1,32,1024]{2,1,0:T(8,128)} %collective-permute-done.3, f32[34]{0:T(128)S(1)} %pad.74.clone), kind=kLoop, calls=%fused_computation.3 | loop fusion | flops 2506752 | bytes 4939912 | tf_op jit(solution)/shard_map/concatenate | solution.py:52
  34.1 4.7 %fusion.5 = f32[16,32,1024]{2,1,0:T(8,128)S(1)} fusion(f32[16,32,1024]{2,1,0:T(8,128)S(1)} %copy-done.7, f32[18,34,1024]{2,1,0:T(8,128)S(1)} %pad_maximum_fusion.2, f32[1,32,1024]{2,1,0:T(8,128)} %collective-permute-done.2, f32[1,32,1024]{2,1,0:T(8,128)} %collective-permute-done.3, f32[18,1,1024]{2,1,0:T(1,128)S(1)} %broadcast_in_dim.48, ...), kind=kLoop, calls=%fused_computation.38 | loop fusion | flops 18874368 | bytes 11231232 | tf_op jit(solution)/shard_map/add | solution.py:78
  38.9 1.3 copy-done.4
  40.9 1.9 %collective-permute-start.4 = (f32[1,32,1024]{2,1,0:T(8,128)}, f32[1,32,1024]{2,1,0:T(8,128)}, u32[]{:S(2)}, u32[]{:S(2)}) collective-permute-start(f32[1,32,1024]{2,1,0:T(8,128)} %get-tuple-element.18), channel_id=1, source_target_pairs={{1,0},{2,1},{3,2},{4,3},{5,4},{6,5},{7,6},{9,8},{10,9},{11,10},{12... | collective-permute-start | bytes 393224 | tf_op jit(solution)/shard_map/ppermute | solution.py:22
  42.8 4.4 %collective-permute-start.5 = (f32[1,32,1024]{2,1,0:T(8,128)}, f32[1,32,1024]{2,1,0:T(8,128)}, u32[]{:S(2)}, u32[]{:S(2)}) collective-permute-start(f32[1,32,1024]{2,1,0:T(8,128)} %get-tuple-element.17), channel_id=1, source_target_pairs={{0,1},{1,2},{2,3},{3,4},{4,5},{5,6},{6,7},{8,9},{9,10},{10,11},{11... | collective-permute-start | bytes 393224 | tf_op jit(solution)/shard_map/ppermute | solution.py:20
  48.1 3.7 %all-to-all-start = ((f32[8,16,128]{2,1,0:T(8,128)}), f32[8,16,128]{2,1,0:T(8,128)S(1)}, u32[]{:S(2)}, u32[]{:S(2)}) async-start(f32[8,16,128]{2,1,0:T(8,128)} %fusion.37), calls=%async_computation | async-start | bytes 131072 | tf_op jit(solution)/shard_map/all_to_all | solution.py:44
  51.8 2.3 %pad_maximum_fusion.1 = f32[18,34,1024]{2,1,0:T(8,128)S(1)} fusion(f32[18,1,1024]{2,1,0:T(1,128)S(1)} %broadcast_in_dim.48, f32[1,32,1024]{2,1,0:T(8,128)} %collective-permute-done.4, f32[16,32,1024]{2,1,0:T(8,128)} %copy-done.4, f32[1,32,1024]{2,1,0:T(8,128)} %collective-permute-done.5, f32[34]{0:T(128)S(1)} %pad.74.clone), kind=kLoop, calls=%fused_computation.2 | loop fusion | flops 2506752 | bytes 4939912 | tf_op jit(solution)/shard_map/concatenate | solution.py:52
  54.4 4.7 %fusion.8 = f32[16,32,1024]{2,1,0:T(8,128)S(1)} fusion(f32[16,32,1024]{2,1,0:T(8,128)S(1)} %copy-done.5, f32[18,34,1024]{2,1,0:T(8,128)S(1)} %pad_maximum_fusion.1, f32[1,32,1024]{2,1,0:T(8,128)} %collective-permute-done.4, f32[1,32,1024]{2,1,0:T(8,128)} %collective-permute-done.5, f32[18,1,1024]{2,1,0:T(1,128)S(1)} %broadcast_in_dim.48, ...), kind=kLoop, calls=%fused_computation.41 | loop fusion | flops 18874368 | bytes 11231232 | tf_op jit(solution)/shard_map/add | solution.py:78
  59.1 1.3 copy-done.2
  61.1 1.9 %collective-permute-start.6 = (f32[1,32,1024]{2,1,0:T(8,128)}, f32[1,32,1024]{2,1,0:T(8,128)}, u32[]{:S(2)}, u32[]{:S(2)}) collective-permute-start(f32[1,32,1024]{2,1,0:T(8,128)} %get-tuple-element.16), channel_id=1, source_target_pairs={{1,0},{2,1},{3,2},{4,3},{5,4},{6,5},{7,6},{9,8},{10,9},{11,10},{12... | collective-permute-start | bytes 393224 | tf_op jit(solution)/shard_map/ppermute | solution.py:22
  63.0 3.6 %collective-permute-start.7 = (f32[1,32,1024]{2,1,0:T(8,128)}, f32[1,32,1024]{2,1,0:T(8,128)}, u32[]{:S(2)}, u32[]{:S(2)}) collective-permute-start(f32[1,32,1024]{2,1,0:T(8,128)} %get-tuple-element.15), channel_id=1, source_target_pairs={{0,1},{1,2},{2,3},{3,4},{4,5},{5,6},{6,7},{8,9},{9,10},{10,11},{11... | collective-permute-start | bytes 393224 | tf_op jit(solution)/shard_map/ppermute | solution.py:20
  68.0 11.3 %all-to-all-start.1 = ((f32[32,16,128]{2,1,0:T(8,128)}), f32[32,16,128]{2,1,0:T(8,128)}, u32[]{:S(2)}, u32[]{:S(2)}) async-start(f32[32,16,128]{2,1,0:T(8,128)} %broadcast_in_dim.51), calls=%async_computation.1 | async-start | bytes 524288 | tf_op jit(solution)/shard_map/all_to_all | solution.py:38
  79.4 2.3 %pad_maximum_fusion = f32[18,34,1024]{2,1,0:T(8,128)S(1)} fusion(f32[18,1,1024]{2,1,0:T(1,128)S(1)} %broadcast_in_dim.48, f32[1,32,1024]{2,1,0:T(8,128)} %collective-permute-done.6, f32[16,32,1024]{2,1,0:T(8,128)} %copy-done.2, f32[1,32,1024]{2,1,0:T(8,128)} %collective-permute-done.7, f32[34]{0:T(128)} %copy-done.20), kind=kLoop, calls=%fused_computation.1 | loop fusion | flops 2506752 | bytes 4939912 | tf_op jit(solution)/shard_map/concatenate | solution.py:52
  81.9 4.7 %fusion.11 = f32[16,32,1024]{2,1,0:T(8,128)S(1)} fusion(f32[16,32,1024]{2,1,0:T(8,128)S(1)} %copy-done.3, f32[18,34,1024]{2,1,0:T(8,128)S(1)} %pad_maximum_fusion, f32[1,32,1024]{2,1,0:T(8,128)} %collective-permute-done.6, f32[1,32,1024]{2,1,0:T(8,128)} %collective-permute-done.7, f32[18,1,1024]{2,1,0:T(1,128)S(1)} %broadcast_in_dim.48, ...), kind=kLoop, calls=%fused_computation.44 | loop fusion | flops 18874368 | bytes 11231232 | tf_op jit(solution)/shard_map/add | solution.py:78
  86.7 1.3 copy-done.12
  88.5 5.3 %collective-permute-start.8 = (f32[1,256]{1,0:T(1,128)S(1)}, f32[1,256]{1,0:T(1,128)S(1)}, u32[]{:S(2)}, u32[]{:S(2)}) collective-permute-start(f32[1,256]{1,0:T(1,128)S(1)} %div.18), channel_id=1, source_target_pairs={{0,128},{8,136},{16,144},{24,152},{32,160},{40,168},{48,176},{56,1... | collective-permute-start | bytes 3080 | tf_op jit(solution)/shard_map/ppermute | solution.py:32
  93.7 1.2 collective-permute-done.8
  95.0 11.7 %all_gather.3 = f32[1,2048]{1,0:T(1,128)S(1)} all-gather(f32[1,256]{1,0:T(1,128)S(1)} %collective-permute-done.8), channel_id=1, replica_groups=mesh['wide'=32,'slab'=8] {'slab'}, dimensions={1}, use_global_device_ids=true | all-gather | bytes 9216 | tf_op jit(solution)/shard_map/all_gather | solution.py:120
  106.6 1.7 %gather_fusion = f32[256]{0:T(256)S(1)} fusion(f32[2048]{0:T(1024)S(1)} %bitcast.101, s32[1024]{0:T(1024)S(1)} %pad_clamp_fusion), kind=kCustom, calls=%fused_computation | custom fusion | bytes 3072 | tf_op jit(solution)/shard_map/jit(_take)/gather | solution.py:121
  110.0 3.4 %all-to-all-start.2 = ((f32[8,16,128]{2,1,0:T(8,128)}), f32[8,16,128]{2,1,0:T(8,128)S(1)}, u32[]{:S(2)}, u32[]{:S(2)}) async-start(f32[8,16,128]{2,1,0:T(8,128)} %broadcast_in_dim.52), calls=%async_computation.2 | async-start | bytes 131072 | tf_op jit(solution)/shard_map/all_to_all | solution.py:47
  113.6 4.7 %all-to-all-done.2 = f32[8,16,128]{2,1,0:T(8,128)S(1)} async-done(((f32[8,16,128]{2,1,0:T(8,128)}), f32[8,16,128]{2,1,0:T(8,128)S(1)}, u32[]{:S(2)}, u32[]{:S(2)}) %all-to-all-start.2) | async-done | bytes 65568 | tf_op jit(solution)/shard_map/all_to_all | solution.py:47
  119.0 11.3 %all-to-all-start.3 = ((f32[256,1,128]{2,1,0:T(1,128)}), f32[256,1,128]{2,1,0:T(1,128)S(1)}, u32[]{:S(2)}, u32[]{:S(2)}) async-start(f32[256,1,128]{2,1,0:T(1,128)} %broadcast_in_dim.54), calls=%async_computation.3 | async-start | bytes 262144 | tf_op jit(solution)/shard_map/all_to_all | solution.py:38
  130.5 11.7 %cholesky.16 = f32[128,128]{1,0:T(8,128)S(1)} custom-call(f32[128,128]{1,0:T(8,128)S(1)} %fusion.45), custom_call_target="Cholesky" | custom-call | tf_op jit(solution)/shard_map/jit(cholesky)/cholesky | solution.py:128
  143.5 9.8 %custom-call.10 = f32[1,128,128]{1,2,0:T(8,128)S(1)} custom-call(f32[1,128,128]{2,1,0:T(8,128)S(1)} %fusion.41), custom_call_target="InvertDiagBlocksLowerTriangular" | custom-call | tf_op jit(solution)/shard_map/triangular_solve | solution.py:132
  (91 shorter events, 16.9 us)
Async XLA Ops:
  0.6 154.2 %copy-start = (f32[1,256,128]{2,1,0:T(8,128)S(1)}, f32[1,256,128]{2,1,0:T(8,128)}, u32[]{:S(2)}) copy-start(f32[1,256,128]{2,1,0:T(8,128)} %param.13) | copy-start | bytes 393220
  1.7 9.3 %collective-permute-start = (f32[1,32,1024]{2,1,0:T(8,128)S(1)}, f32[1,32,1024]{2,1,0:T(8,128)S(1)}, u32[]{:S(2)}, u32[]{:S(2)}) collective-permute-start(f32[1,32,1024]{2,1,0:T(8,128)S(1)} %get-tuple-element.22), channel_id=1, source_target_pairs={{1,0},{2,1},{3,2},{4,3},{5,4},{6,5},{7,6},{9,8},{10,9},{11,10},{12... | collective-permute-start | bytes 393224 | tf_op jit(solution)/shard_map/ppermute | solution.py:22
  6.8 4.2 %collective-permute-start.1 = (f32[1,32,1024]{2,1,0:T(8,128)S(1)}, f32[1,32,1024]{2,1,0:T(8,128)S(1)}, u32[]{:S(2)}, u32[]{:S(2)}) collective-permute-start(f32[1,32,1024]{2,1,0:T(8,128)S(1)} %get-tuple-element.21), channel_id=1, source_target_pairs={{0,1},{1,2},{2,3},{3,4},{4,5},{5,6},{6,7},{8,9},{9,10},{10,11},{11... | collective-permute-start | bytes 393224 | tf_op jit(solution)/shard_map/ppermute | solution.py:20
  11.0 40.8 %copy-start.20 = (f32[34]{0:T(128)}, f32[34]{0:T(128)S(1)}, u32[]{:S(2)}) copy-start(f32[34]{0:T(128)S(1)} %pad.74.clone) | copy-start | bytes 412
  11.7 2.6 %copy-start.1 = (bf16[3,1,16,32,1024]{4,3,2,1,0:T(8,128)(2,1)S(1)}, bf16[3,1,16,32,1024]{4,3,2,1,0:T(8,128)(2,1)}, u32[]{:S(2)}) copy-start(bf16[3,1,16,32,1024]{4,3,2,1,0:T(8,128)(2,1)} %param.9) | copy-start | bytes 9437188
  11.7 2.8 %copy-start.8 = (bf16[1,16,32,1024]{3,2,1,0:T(8,128)(2,1)S(1)}, bf16[1,16,32,1024]{3,2,1,0:T(8,128)(2,1)}, u32[]{:S(2)}) copy-start(bf16[1,16,32,1024]{3,2,1,0:T(8,128)(2,1)} %param.8) | copy-start | bytes 3145732
  11.7 2.8 %copy-start.16 = (f32[1,32,1024]{2,1,0:T(8,128)S(1)}, f32[1,32,1024]{2,1,0:T(8,128)}, u32[]{:S(2)}) copy-start(f32[1,32,1024]{2,1,0:T(8,128)} %copy-done.15) | copy-start | bytes 393220
  14.6 15.1 %copy-start.13 = (f32[1,256,128]{2,1,0:T(8,128)S(1)}, f32[1,256,128]{2,1,0:T(8,128)}, u32[]{:S(2)}) copy-start(f32[1,256,128]{2,1,0:T(8,128)} %param.12) | copy-start | bytes 393220
  21.7 1.3 copy-start.6
  23.7 6.9 %collective-permute-start.2 = (f32[1,32,1024]{2,1,0:T(8,128)}, f32[1,32,1024]{2,1,0:T(8,128)}, u32[]{:S(2)}, u32[]{:S(2)}) collective-permute-start(f32[1,32,1024]{2,1,0:T(8,128)} %get-tuple-element.20), channel_id=1, source_target_pairs={{1,0},{2,1},{3,2},{4,3},{5,4},{6,5},{7,6},{9,8},{10,9},{11,10},{12... | collective-permute-start | bytes 393224 | tf_op jit(solution)/shard_map/ppermute | solution.py:22
  26.1 5.7 %collective-permute-start.3 = (f32[1,32,1024]{2,1,0:T(8,128)}, f32[1,32,1024]{2,1,0:T(8,128)}, u32[]{:S(2)}, u32[]{:S(2)}) collective-permute-start(f32[1,32,1024]{2,1,0:T(8,128)} %get-tuple-element.19), channel_id=1, source_target_pairs={{0,1},{1,2},{2,3},{3,4},{4,5},{5,6},{6,7},{8,9},{9,10},{10,11},{11... | collective-permute-start | bytes 393224 | tf_op jit(solution)/shard_map/ppermute | solution.py:20
  30.4 3.7 %copy-start.7 = (f32[16,32,1024]{2,1,0:T(8,128)S(1)}, f32[16,32,1024]{2,1,0:T(8,128)}, u32[]{:S(2)}) copy-start(f32[16,32,1024]{2,1,0:T(8,128)} %copy-done.6) | copy-start | bytes 6291460
  30.4 3.7 %copy-start.9 = (bf16[1,16,32,1024]{3,2,1,0:T(8,128)(2,1)S(1)}, bf16[1,16,32,1024]{3,2,1,0:T(8,128)(2,1)}, u32[]{:S(2)}) copy-start(bf16[1,16,32,1024]{3,2,1,0:T(8,128)(2,1)} %param.8) | copy-start | bytes 3145732
  34.1 13.1 %copy-start.17 = (f32[1,256,128]{1,2,0:T(8,128)S(1)}, f32[1,256,128]{1,2,0:T(8,128)}, u32[]{:S(2)}) copy-start(f32[1,256,128]{1,2,0:T(8,128)} %copy.21) | copy-start | bytes 393220
  38.8 1.3 copy-start.4
  40.9 10.9 %collective-permute-start.4 = (f32[1,32,1024]{2,1,0:T(8,128)}, f32[1,32,1024]{2,1,0:T(8,128)}, u32[]{:S(2)}, u32[]{:S(2)}) collective-permute-start(f32[1,32,1024]{2,1,0:T(8,128)} %get-tuple-element.18), channel_id=1, source_target_pairs={{1,0},{2,1},{3,2},{4,3},{5,4},{6,5},{7,6},{9,8},{10,9},{11,10},{12... | collective-permute-start | bytes 393224 | tf_op jit(solution)/shard_map/ppermute | solution.py:22
  42.8 9.0 %collective-permute-start.5 = (f32[1,32,1024]{2,1,0:T(8,128)}, f32[1,32,1024]{2,1,0:T(8,128)}, u32[]{:S(2)}, u32[]{:S(2)}) collective-permute-start(f32[1,32,1024]{2,1,0:T(8,128)} %get-tuple-element.17), channel_id=1, source_target_pairs={{0,1},{1,2},{2,3},{3,4},{4,5},{5,6},{6,7},{8,9},{9,10},{10,11},{11... | collective-permute-start | bytes 393224 | tf_op jit(solution)/shard_map/ppermute | solution.py:20
  48.1 19.2 %all-to-all-start = ((f32[8,16,128]{2,1,0:T(8,128)}), f32[8,16,128]{2,1,0:T(8,128)S(1)}, u32[]{:S(2)}, u32[]{:S(2)}) async-start(f32[8,16,128]{2,1,0:T(8,128)} %fusion.37), calls=%async_computation | async-start | bytes 131072 | tf_op jit(solution)/shard_map/all_to_all | solution.py:44
  51.8 2.4 %copy-start.5 = (f32[16,32,1024]{2,1,0:T(8,128)S(1)}, f32[16,32,1024]{2,1,0:T(8,128)}, u32[]{:S(2)}) copy-start(f32[16,32,1024]{2,1,0:T(8,128)} %copy-done.4) | copy-start | bytes 6291460
  51.8 2.6 %copy-start.10 = (bf16[1,16,32,1024]{3,2,1,0:T(8,128)(2,1)S(1)}, bf16[1,16,32,1024]{3,2,1,0:T(8,128)(2,1)}, u32[]{:S(2)}) copy-start(bf16[1,16,32,1024]{3,2,1,0:T(8,128)(2,1)} %param.8) | copy-start | bytes 3145732
  54.4 12.3 %copy-start.18 = (s32[1,256]{1,0:T(1,128)S(1)}, s32[1,256]{1,0:T(1,128)}, u32[]{:S(2)}) copy-start(s32[1,256]{1,0:T(1,128)} %param.11) | copy-start | bytes 3076
  61.1 18.2 %collective-permute-start.6 = (f32[1,32,1024]{2,1,0:T(8,128)}, f32[1,32,1024]{2,1,0:T(8,128)}, u32[]{:S(2)}, u32[]{:S(2)}) collective-permute-start(f32[1,32,1024]{2,1,0:T(8,128)} %get-tuple-element.16), channel_id=1, source_target_pairs={{1,0},{2,1},{3,2},{4,3},{5,4},{6,5},{7,6},{9,8},{10,9},{11,10},{12... | collective-permute-start | bytes 393224 | tf_op jit(solution)/shard_map/ppermute | solution.py:22
  63.0 16.3 %collective-permute-start.7 = (f32[1,32,1024]{2,1,0:T(8,128)}, f32[1,32,1024]{2,1,0:T(8,128)}, u32[]{:S(2)}, u32[]{:S(2)}) collective-permute-start(f32[1,32,1024]{2,1,0:T(8,128)} %get-tuple-element.15), channel_id=1, source_target_pairs={{0,1},{1,2},{2,3},{3,4},{4,5},{5,6},{6,7},{8,9},{9,10},{10,11},{11... | collective-permute-start | bytes 393224 | tf_op jit(solution)/shard_map/ppermute | solution.py:20
  68.0 40.4 %all-to-all-start.1 = ((f32[32,16,128]{2,1,0:T(8,128)}), f32[32,16,128]{2,1,0:T(8,128)}, u32[]{:S(2)}, u32[]{:S(2)}) async-start(f32[32,16,128]{2,1,0:T(8,128)} %broadcast_in_dim.51), calls=%async_computation.1 | async-start | bytes 524288 | tf_op jit(solution)/shard_map/all_to_all | solution.py:38
  79.3 2.4 %copy-start.3 = (f32[16,32,1024]{2,1,0:T(8,128)S(1)}, f32[16,32,1024]{2,1,0:T(8,128)}, u32[]{:S(2)}) copy-start(f32[16,32,1024]{2,1,0:T(8,128)} %copy-done.2) | copy-start | bytes 6291460
  79.4 2.6 %copy-start.11 = (bf16[1,16,32,1024]{3,2,1,0:T(8,128)(2,1)S(1)}, bf16[1,16,32,1024]{3,2,1,0:T(8,128)(2,1)}, u32[]{:S(2)}) copy-start(bf16[1,16,32,1024]{3,2,1,0:T(8,128)(2,1)} %param.8) | copy-start | bytes 3145732
  81.9 11.8 %copy-start.22 = (s32[256,1]{0,1:T(1,128)S(1)}, s32[256,1]{0,1:T(1,128)}, u32[]{:S(2)}) copy-start(s32[256,1]{0,1:T(1,128)} %compare_select_fusion.1) | copy-start | bytes 3076
  81.9 31.5 %copy-start.19 = (s32[1,256]{1,0:T(1,128)S(1)}, s32[1,256]{1,0:T(1,128)}, u32[]{:S(2)}) copy-start(s32[1,256]{1,0:T(1,128)} %param.11) | copy-start | bytes 3076
  81.9 31.5 %copy-start.21 = (f32[1,256]{1,0:T(1,128)S(1)}, f32[1,256]{1,0:T(1,128)}, u32[]{:S(2)}) copy-start(f32[1,256]{1,0:T(1,128)} %param.10) | copy-start | bytes 3076
  88.5 6.5 %collective-permute-start.8 = (f32[1,256]{1,0:T(1,128)S(1)}, f32[1,256]{1,0:T(1,128)S(1)}, u32[]{:S(2)}, u32[]{:S(2)}) collective-permute-start(f32[1,256]{1,0:T(1,128)S(1)} %div.18), channel_id=1, source_target_pairs={{0,128},{8,136},{16,144},{24,152},{32,160},{40,168},{48,176},{56,1... | collective-permute-start | bytes 3080 | tf_op jit(solution)/shard_map/ppermute | solution.py:32
  110.0 8.3 %all-to-all-start.2 = ((f32[8,16,128]{2,1,0:T(8,128)}), f32[8,16,128]{2,1,0:T(8,128)S(1)}, u32[]{:S(2)}, u32[]{:S(2)}) async-start(f32[8,16,128]{2,1,0:T(8,128)} %broadcast_in_dim.52), calls=%async_computation.2 | async-start | bytes 131072 | tf_op jit(solution)/shard_map/all_to_all | solution.py:47
  119.0 35.4 %all-to-all-start.3 = ((f32[256,1,128]{2,1,0:T(1,128)}), f32[256,1,128]{2,1,0:T(1,128)S(1)}, u32[]{:S(2)}, u32[]{:S(2)}) async-start(f32[256,1,128]{2,1,0:T(1,128)} %broadcast_in_dim.54), calls=%async_computation.3 | async-start | bytes 262144 | tf_op jit(solution)/shard_map/all_to_all | solution.py:38
  (4 other events, 4.0 us)
where the time goes:
time: 156 us
  starting transfers between devices  59.9 us (38%)
  other arithmetic  56.9 us (36%)
  local copies, waits for them, and re-layouts  16.7 us (11%)
  blocking collectives  11.7 us (8%)
  waiting for transfers between devices  7.42 us (5%)
  matrix products  1.95 us (1%)
    all_to_all x2, starting transfers between devices, gather_sum(): return jnp.sum(lax.all_to_all(copies, axes, 0, 0, tiled=True), axis=0)  22.6 us
    add x4, other arithmetic, march_forward(): centre + STEP_SIZE * (diffuse_subdomain.astype(jnp.float32) * spread - ca...  21.2 us
    ppermute x4, starting transfers between devices, padded(): lax.ppermute(tail, axis, [(i, (i + 1) % count) for i in range(ends)])  13.4 us
    another operation x3, other arithmetic, shards(): lower_factor = jnp.linalg.cholesky(gram_matrix)  12.4 us
    all_gather x1, blocking collectives, shards(): partner_all = lax.all_gather(partner_own, 'slab', axis=1, tiled=True)  11.7 us
    ppermute x4, starting transfers between devices, padded(): lax.ppermute(head, axis, [((i + 1) % count, i) for i in range(ends)])  11.4 us
    another operation x2, other arithmetic, shards(): lax.linalg.triangular_solve(lower_factor, half_solve, left_side=True, low...  10.5 us
    concatenate x4, other arithmetic, surround_wrapper(): jnp.concatenate([bottom, block_rows, mirror_layer[:, None, :]], axis=1)  9.12 us
  transfers between devices with their start and end apart: 13, of which 4 were waited for; matrix products, arithmetic and copies ran while one was open for 30% of the time, Pallas kernels for 0%

commit v1 on v0

--- a/solution.py
+++ b/solution.py
@@ -7,6 +7,19 @@
 INTERFACE_STRIP = 64
 SWEEPS = 4
 STEP_SIZE = 0.11
+
+
+def gather_around(array, axis, dim):
+    ways = lax.axis_size(axis)
+    up = [(d, (d + 1) % ways) for d in range(ways)]
+    down = [(d, (d - 1) % ways) for d in range(ways)]
+    earlier, later = ([array], [array])
+    for _ in range(ways // 2):
+        earlier.append(lax.ppermute(earlier[-1], axis, up))
+    for _ in range((ways - 1) // 2):
+        later.append(lax.ppermute(later[-1], axis, down))
+    line = jnp.concatenate([*earlier[::-1], *later[1:]], axis=dim)
+    return jnp.roll(line, (lax.axis_index(axis) - ways // 2) * array.shape[dim], axis=dim)
 
 
 def padded(cells, sides, width):
@@ -117,7 +130,7 @@
     face_means = face_means.reshape(1, rows_dev)
     top_bit = lax.axis_size("wide").bit_length() - 2
     partner_own = partner(face_means, "wide", top_bit)
-    partner_all = lax.all_gather(partner_own, "slab", axis=1, tiled=True)
+    partner_all = gather_around(partner_own, "slab", 1)
     tilde = jnp.take(partner_all[0], partner_facing_rows[0], axis=0)
     resid = tilde - interface_guess[0]
     proj_local = jnp.dot(

time: 156 us -> 152 us (0.974)
  waiting for transfers between devices: 7.42 us -> 19.7 us
  blocking collectives: 11.7 us -> 0 us
  starting transfers between devices: 59.9 us -> 69.8 us
  local copies, waits for them, and re-layouts: 16.7 us -> 7.8 us
  other arithmetic: 56.9 us -> 50.9 us
    all_gather x1 -> x0, blocking collectives: 11.7 us -> none  [shards(): partner_all = lax.all_gather(partner_own, 'slab', axis=1, tiled=True)]
    ppermute x0 -> x7, starting transfers between devices: none -> 11 us  [the longest x4 9.48 us: gather_around(): earlier.append(lax.ppermute(earlier[-1], axis, up))]
    unnamed x49 -> x34, local copies, waits for them, and re-layouts: 8.98 us -> 2.01 us
    all_to_all x2, starting transfers between devices: 22.6 us -> 15.7 us  [gather_sum(): return jnp.sum(lax.all_to_all(copies, axes, 0, 0, tiled=True), axis=0)]
    all_to_all x2, waiting for transfers between devices: 0.01 us -> 5.74 us  [gather_sum(): return jnp.sum(lax.all_to_all(copies, axes, 0, 0, tiled=True), axis=0)]
    concatenate x4, other arithmetic: 9.12 us -> 4.21 us  [surround_wrapper(): jnp.concatenate([bottom, block_rows, mirror_layer[:, None, :]], axis=1)]
    all_to_all x1, starting transfers between devices: 3.44 us -> 6.7 us  [sum_everywhere(): lax.all_to_all(copies, 'slab', 0, 0, tiled=True).reshape(square.shape)]
    ppermute x0 -> x7, waiting for transfers between devices: none -> 2.83 us  [the longest x3 1.69 us: gather_around(): later.append(lax.ppermute(later[-1], axis, down))]
  transfers between devices with their start and end apart: 13 -> 20, of which waited for: 4 -> 13; matrix products, arithmetic and copies ran while one was open for 30% -> 20% of each run, Pallas kernels for 0% -> 0%
where the time goes in v1:
time: 152 us; the launch traced here: 151 us
  starting transfers between devices  69.8 us (46%)
  other arithmetic  50.9 us (33%)
  waiting for transfers between devices  19.7 us (13%)
  local copies, waits for them, and re-layouts  7.8 us (5%)
  matrix products  1.96 us (1%)
    add x4, other arithmetic, march_forward(): centre + STEP_SIZE * (diffuse_subdomain.astype(jnp.float32) * spread - ca...  21.7 us
    all_to_all x2, starting transfers between devices, gather_sum(): return jnp.sum(lax.all_to_all(copies, axes, 0, 0, tiled=True), axis=0)  15.7 us
    ppermute x4, starting transfers between devices, padded(): lax.ppermute(tail, axis, [(i, (i + 1) % count) for i in range(ends)])  14.3 us
    another operation x3, other arithmetic, shards(): lower_factor = jnp.linalg.cholesky(gram_matrix)  12.4 us
    ppermute x4, starting transfers between devices, padded(): lax.ppermute(head, axis, [((i + 1) % count, i) for i in range(ends)])  11.4 us
    another operation x2, other arithmetic, shards(): lax.linalg.triangular_solve(lower_factor, half_solve, left_side=True, low...  10.5 us
    ppermute x4, starting transfers between devices, gather_around(): earlier.append(lax.ppermute(earlier[-1], axis, up))  9.48 us
    all_to_all x1, starting transfers between devices, sum_everywhere(): lax.all_to_all(copies, 'slab', 0, 0, tiled=True).reshape(square.shape)  6.7 us
  transfers between devices with their start and end apart: 20, of which 13 were waited for; matrix products, arithmetic and copies ran while one was open for 20% of the time, Pallas kernels for 0%

profile of v1, /device:TPU:1, one launch (start us, length us, event | category | flops | bytes accessed | tf_op | source)
XLA Modules:
  0.0 151.3 jit_solution(6239049017597496087)
XLA Ops:
  1.8 5.1 %collective-permute-start = (f32[1,32,1024]{2,1,0:T(8,128)S(1)}, f32[1,32,1024]{2,1,0:T(8,128)S(1)}, u32[]{:S(2)}, u32[]{:S(2)}) collective-permute-start(f32[1,32,1024]{2,1,0:T(8,128)S(1)} %get-tuple-element.22), channel_id=1, source_target_pairs={{1,0},{2,1},{3,2},{4,3},{5,4},{6,5},{7,6},{9,8},{10,9},{11,10},{12... | collective-permute-start | bytes 393224 | tf_op jit(solution)/shard_map/ppermute | solution.py:35
  7.0 1.9 %collective-permute-start.1 = (f32[1,32,1024]{2,1,0:T(8,128)S(1)}, f32[1,32,1024]{2,1,0:T(8,128)S(1)}, u32[]{:S(2)}, u32[]{:S(2)}) collective-permute-start(f32[1,32,1024]{2,1,0:T(8,128)S(1)} %get-tuple-element.21), channel_id=1, source_target_pairs={{0,1},{1,2},{2,3},{3,4},{4,5},{5,6},{6,7},{8,9},{9,10},{10,11},{11... | collective-permute-start | bytes 393224 | tf_op jit(solution)/shard_map/ppermute | solution.py:33
  9.4 1.3 reduce.12
  11.2 2.3 %pad_maximum_fusion.3 = f32[18,34,1024]{2,1,0:T(8,128)S(1)} fusion(f32[18,1,1024]{2,1,0:T(1,128)S(1)} %broadcast_in_dim.48, f32[1,32,1024]{2,1,0:T(8,128)S(1)} %collective-permute-done, f32[16,32,1024]{2,1,0:T(8,128)} %bitcast.102, f32[1,32,1024]{2,1,0:T(8,128)S(1)} %collective-permute-done.1, f32[34]{0:T(128)S(1)} %pad.74.clone), kind=kLoop, calls=%fused_computation.4 | loop fusion | flops 2506752 | bytes 4939912 | tf_op jit(solution)/shard_map/concatenate | solution.py:65
  13.9 5.4 %fusion.2 = f32[16,32,1024]{2,1,0:T(8,128)S(1)} fusion(f32[16,32,1024]{2,1,0:T(8,128)S(1)} %bitcast.103, f32[18,34,1024]{2,1,0:T(8,128)S(1)} %pad_maximum_fusion.3, f32[1,32,1024]{2,1,0:T(8,128)S(1)} %collective-permute-done, f32[1,32,1024]{2,1,0:T(8,128)S(1)} %collective-permute-done.1, f32[18,1,1024]{2,1,0:T(1,128)S(1)} %broadcast_in_dim.48, ...), kind=kLoop, calls=%fused_computation.35 | loop fusion | flops 18874368 | bytes 11231232 | tf_op jit(solution)/shard_map/add | solution.py:91
  19.4 2.4 %collective-permute-start.2 = (f32[1,32,1024]{2,1,0:T(8,128)S(1)}, f32[1,32,1024]{2,1,0:T(8,128)S(1)}, u32[]{:S(2)}, u32[]{:S(2)}) collective-permute-start(f32[1,32,1024]{2,1,0:T(8,128)S(1)} %get-tuple-element.20), channel_id=1, source_target_pairs={{1,0},{2,1},{3,2},{4,3},{5,4},{6,5},{7,6},{9,8},{10,9},{11,10},{12... | collective-permute-start | bytes 393224 | tf_op jit(solution)/shard_map/ppermute | solution.py:35
  21.8 3.5 %collective-permute-start.3 = (f32[1,32,1024]{2,1,0:T(8,128)S(1)}, f32[1,32,1024]{2,1,0:T(8,128)S(1)}, u32[]{:S(2)}, u32[]{:S(2)}) collective-permute-start(f32[1,32,1024]{2,1,0:T(8,128)S(1)} %get-tuple-element.19), channel_id=1, source_target_pairs={{0,1},{1,2},{2,3},{3,4},{4,5},{5,6},{6,7},{8,9},{9,10},{10,11},{11... | collective-permute-start | bytes 393224 | tf_op jit(solution)/shard_map/ppermute | solution.py:33
  26.1 1.2 collective-permute-done.3
  27.9 5.4 %fusion.5 = f32[16,32,1024]{2,1,0:T(8,128)S(1)} fusion(f32[16,32,1024]{2,1,0:T(8,128)S(1)} %fusion.2, f32[18,34,1024]{2,1,0:T(8,128)S(1)} %pad_maximum_fusion.2, f32[1,32,1024]{2,1,0:T(8,128)S(1)} %collective-permute-done.2, f32[1,32,1024]{2,1,0:T(8,128)S(1)} %collective-permute-done.3, f32[18,1,1024]{2,1,0:T(1,128)S(1)} %broadcast_in_dim.48, ...), kind=kLoop, calls=%fused_computation.38 | loop fusion | flops 18874368 | bytes 11231232 | tf_op jit(solution)/shard_map/add | solution.py:91
  33.4 1.9 %collective-permute-start.4 = (f32[1,32,1024]{2,1,0:T(8,128)S(1)}, f32[1,32,1024]{2,1,0:T(8,128)S(1)}, u32[]{:S(2)}, u32[]{:S(2)}) collective-permute-start(f32[1,32,1024]{2,1,0:T(8,128)S(1)} %get-tuple-element.18), channel_id=1, source_target_pairs={{1,0},{2,1},{3,2},{4,3},{5,4},{6,5},{7,6},{9,8},{10,9},{11,10},{12... | collective-permute-start | bytes 393224 | tf_op jit(solution)/shard_map/ppermute | solution.py:35
  35.3 4.4 %collective-permute-start.5 = (f32[1,32,1024]{2,1,0:T(8,128)S(1)}, f32[1,32,1024]{2,1,0:T(8,128)S(1)}, u32[]{:S(2)}, u32[]{:S(2)}) collective-permute-start(f32[1,32,1024]{2,1,0:T(8,128)S(1)} %get-tuple-element.17), channel_id=1, source_target_pairs={{0,1},{1,2},{2,3},{3,4},{4,5},{5,6},{6,7},{8,9},{9,10},{10,11},{11... | collective-permute-start | bytes 393224 | tf_op jit(solution)/shard_map/ppermute | solution.py:33
  40.4 1.2 collective-permute-done.5
  42.3 5.4 %fusion.8 = f32[16,32,1024]{2,1,0:T(8,128)S(1)} fusion(f32[16,32,1024]{2,1,0:T(8,128)S(1)} %fusion.5, f32[18,34,1024]{2,1,0:T(8,128)S(1)} %pad_maximum_fusion.1, f32[1,32,1024]{2,1,0:T(8,128)S(1)} %collective-permute-done.4, f32[1,32,1024]{2,1,0:T(8,128)S(1)} %collective-permute-done.5, f32[18,1,1024]{2,1,0:T(1,128)S(1)} %broadcast_in_dim.48, ...), kind=kLoop, calls=%fused_computation.41 | loop fusion | flops 18874368 | bytes 11231232 | tf_op jit(solution)/shard_map/add | solution.py:91
  47.7 1.9 %collective-permute-start.6 = (f32[1,32,1024]{2,1,0:T(8,128)S(1)}, f32[1,32,1024]{2,1,0:T(8,128)S(1)}, u32[]{:S(2)}, u32[]{:S(2)}) collective-permute-start(f32[1,32,1024]{2,1,0:T(8,128)S(1)} %get-tuple-element.16), channel_id=1, source_target_pairs={{1,0},{2,1},{3,2},{4,3},{5,4},{6,5},{7,6},{9,8},{10,9},{11,10},{12... | collective-permute-start | bytes 393224 | tf_op jit(solution)/shard_map/ppermute | solution.py:35
  49.6 4.5 %collective-permute-start.7 = (f32[1,32,1024]{2,1,0:T(8,128)S(1)}, f32[1,32,1024]{2,1,0:T(8,128)S(1)}, u32[]{:S(2)}, u32[]{:S(2)}) collective-permute-start(f32[1,32,1024]{2,1,0:T(8,128)S(1)} %get-tuple-element.15), channel_id=1, source_target_pairs={{0,1},{1,2},{2,3},{3,4},{4,5},{5,6},{6,7},{8,9},{9,10},{10,11},{11... | collective-permute-start | bytes 393224 | tf_op jit(solution)/shard_map/ppermute | solution.py:33
  56.6 5.4 %fusion.11 = f32[16,32,1024]{2,1,0:T(8,128)S(1)} fusion(f32[16,32,1024]{2,1,0:T(8,128)S(1)} %fusion.8, f32[18,34,1024]{2,1,0:T(8,128)S(1)} %pad_maximum_fusion, f32[1,32,1024]{2,1,0:T(8,128)S(1)} %collective-permute-done.6, f32[1,32,1024]{2,1,0:T(8,128)S(1)} %collective-permute-done.7, f32[18,1,1024]{2,1,0:T(1,128)S(1)} %broadcast_in_dim.48, ...), kind=kLoop, calls=%fused_computation.44 | loop fusion | flops 18874368 | bytes 11231232 | tf_op jit(solution)/shard_map/add | solution.py:91
  62.5 6.3 %collective-permute-start.8 = (f32[1,256]{1,0:T(1,128)S(1)}, f32[1,256]{1,0:T(1,128)S(1)}, u32[]{:S(2)}, u32[]{:S(2)}) collective-permute-start(f32[1,256]{1,0:T(1,128)S(1)} %div.18), channel_id=1, source_target_pairs={{0,128},{8,136},{16,144},{24,152},{32,160},{40,168},{48,176},{56,1... | collective-permute-start | bytes 3080 | tf_op jit(solution)/shard_map/ppermute | solution.py:45
  69.8 3.3 %collective-permute-start.9 = (f32[1,256]{1,0:T(1,128)S(1)}, f32[1,256]{1,0:T(1,128)S(1)}, u32[]{:S(2)}, u32[]{:S(2)}) collective-permute-start(f32[1,256]{1,0:T(1,128)S(1)} %collective-permute-done.8), channel_id=1, source_target_pairs={{0,1},{1,2},{2,3},{3,4},{4,5},{5,6},{6,7},{7,0},{8,9},{9,10},{10,1... | collective-permute-start | bytes 3080 | tf_op jit(solution)/shard_map/ppermute | solution.py:18
  74.0 4.4 %all-to-all-start = ((f32[8,16,128]{2,1,0:T(8,128)}), f32[8,16,128]{2,1,0:T(8,128)S(1)}, u32[]{:S(2)}, u32[]{:S(2)}) async-start(f32[8,16,128]{2,1,0:T(8,128)} %fusion.37), calls=%async_computation | async-start | bytes 131072 | tf_op jit(solution)/shard_map/all_to_all | solution.py:57
  78.4 1.6 %collective-permute-start.10 = (f32[1,256]{1,0:T(1,128)S(1)}, f32[1,256]{1,0:T(1,128)S(1)}, u32[]{:S(2)}, u32[]{:S(2)}) collective-permute-start(f32[1,256]{1,0:T(1,128)S(1)} %collective-permute-done.9), channel_id=1, source_target_pairs={{0,1},{1,2},{2,3},{3,4},{4,5},{5,6},{6,7},{7,0},{8,9},{9,10},{10,1... | collective-permute-start | bytes 3080 | tf_op jit(solution)/shard_map/ppermute | solution.py:18
  80.7 2.3 %collective-permute-start.11 = (f32[1,256]{1,0:T(1,128)S(1)}, f32[1,256]{1,0:T(1,128)S(1)}, u32[]{:S(2)}, u32[]{:S(2)}) collective-permute-start(f32[1,256]{1,0:T(1,128)S(1)} %collective-permute-done.10), channel_id=1, source_target_pairs={{0,1},{1,2},{2,3},{3,4},{4,5},{5,6},{6,7},{7,0},{8,9},{9,10},{10,1... | collective-permute-start | bytes 3080 | tf_op jit(solution)/shard_map/ppermute | solution.py:18
  83.7 2.3 %collective-permute-start.12 = (f32[1,256]{1,0:T(1,128)S(1)}, f32[1,256]{1,0:T(1,128)S(1)}, u32[]{:S(2)}, u32[]{:S(2)}) collective-permute-start(f32[1,256]{1,0:T(1,128)S(1)} %collective-permute-done.11), channel_id=1, source_target_pairs={{0,1},{1,2},{2,3},{3,4},{4,5},{5,6},{6,7},{7,0},{8,9},{9,10},{10,1... | collective-permute-start | bytes 3080 | tf_op jit(solution)/shard_map/ppermute | solution.py:18
  86.7 9.9 %all-to-all-start.1 = ((f32[32,16,128]{2,1,0:T(8,128)}), f32[32,16,128]{2,1,0:T(8,128)S(1)}, u32[]{:S(2)}, u32[]{:S(2)}) async-start(f32[32,16,128]{2,1,0:T(8,128)} %broadcast_in_dim.51), calls=%async_computation.1 | async-start | bytes 524288 | tf_op jit(solution)/shard_map/all_to_all | solution.py:51
  96.7 1.5 %collective-permute-start.15 = (f32[1,256]{1,0:T(1,128)S(1)}, f32[1,256]{1,0:T(1,128)S(1)}, u32[]{:S(2)}, u32[]{:S(2)}) collective-permute-start(f32[1,256]{1,0:T(1,128)S(1)} %collective-permute-done.14), channel_id=1, source_target_pairs={{0,7},{1,0},{2,1},{3,2},{4,3},{5,4},{6,5},{7,6},{8,15},{9,8},{10,9... | collective-permute-start | bytes 3080 | tf_op jit(solution)/shard_map/ppermute | solution.py:20
  98.3 1.4 collective-permute-done.15
  99.8 1.7 %gather_fusion = f32[256]{0:T(256)S(1)} fusion(f32[2048]{0:T(1024)S(1)} %bitcast.101, s32[1024]{0:T(1024)S(1)} %pad_clamp_fusion), kind=kCustom, calls=%fused_computation | custom fusion | bytes 3072 | tf_op jit(solution)/shard_map/jit(_take)/gather | solution.py:134
  101.5 5.7 %all-to-all-done.1 = f32[32,16,128]{2,1,0:T(8,128)S(1)} async-done(((f32[32,16,128]{2,1,0:T(8,128)}), f32[32,16,128]{2,1,0:T(8,128)S(1)}, u32[]{:S(2)}, u32[]{:S(2)}) %all-to-all-start.1) | async-done | bytes 262176 | tf_op jit(solution)/shard_map/all_to_all | solution.py:51
  108.0 6.7 %all-to-all-start.2 = ((f32[8,16,128]{2,1,0:T(8,128)}), f32[8,16,128]{2,1,0:T(8,128)S(1)}, u32[]{:S(2)}, u32[]{:S(2)}) async-start(f32[8,16,128]{2,1,0:T(8,128)} %broadcast_in_dim.52), calls=%async_computation.2 | async-start | bytes 131072 | tf_op jit(solution)/shard_map/all_to_all | solution.py:60
  114.8 4.7 %all-to-all-done.2 = f32[8,16,128]{2,1,0:T(8,128)S(1)} async-done(((f32[8,16,128]{2,1,0:T(8,128)}), f32[8,16,128]{2,1,0:T(8,128)S(1)}, u32[]{:S(2)}, u32[]{:S(2)}) %all-to-all-start.2) | async-done | bytes 65568 | tf_op jit(solution)/shard_map/all_to_all | solution.py:60
  120.2 5.8 %all-to-all-start.3 = ((f32[256,1,128]{2,1,0:T(1,128)}), f32[256,1,128]{2,1,0:T(1,128)S(1)}, u32[]{:S(2)}, u32[]{:S(2)}) async-start(f32[256,1,128]{2,1,0:T(1,128)} %broadcast_in_dim.54), calls=%async_computation.3 | async-start | bytes 262144 | tf_op jit(solution)/shard_map/all_to_all | solution.py:51
  126.1 11.7 %cholesky.16 = f32[128,128]{1,0:T(8,128)S(1)} custom-call(f32[128,128]{1,0:T(8,128)S(1)} %fusion.45), custom_call_target="Cholesky" | custom-call | tf_op jit(solution)/shard_map/jit(cholesky)/cholesky | solution.py:141
  139.2 9.8 %custom-call.10 = f32[1,128,128]{1,2,0:T(8,128)S(1)} custom-call(f32[1,128,128]{2,1,0:T(8,128)S(1)} %fusion.41), custom_call_target="InvertDiagBlocksLowerTriangular" | custom-call | tf_op jit(solution)/shard_map/triangular_solve | solution.py:145
  (91 shorter events, 17.6 us)
Async XLA Ops:
  0.6 149.8 %copy-start = (f32[1,256,128]{2,1,0:T(8,128)S(1)}, f32[1,256,128]{2,1,0:T(8,128)}, u32[]{:S(2)}) copy-start(f32[1,256,128]{2,1,0:T(8,128)} %param.13) | copy-start | bytes 393220
  0.6 12.8 %copy-start.3 = (f32[1,16,32,1024]{3,2,1,0:T(8,128)S(1)}, f32[1,16,32,1024]{3,2,1,0:T(8,128)}, u32[]{:S(2)}) copy-start(f32[1,16,32,1024]{3,2,1,0:T(8,128)} %param.7) | copy-start | bytes 6291460
  1.8 9.3 %collective-permute-start = (f32[1,32,1024]{2,1,0:T(8,128)S(1)}, f32[1,32,1024]{2,1,0:T(8,128)S(1)}, u32[]{:S(2)}, u32[]{:S(2)}) collective-permute-start(f32[1,32,1024]{2,1,0:T(8,128)S(1)} %get-tuple-element.22), channel_id=1, source_target_pairs={{1,0},{2,1},{3,2},{4,3},{5,4},{6,5},{7,6},{9,8},{10,9},{11,10},{12... | collective-permute-start | bytes 393224 | tf_op jit(solution)/shard_map/ppermute | solution.py:35
  7.0 4.2 %collective-permute-start.1 = (f32[1,32,1024]{2,1,0:T(8,128)S(1)}, f32[1,32,1024]{2,1,0:T(8,128)S(1)}, u32[]{:S(2)}, u32[]{:S(2)}) collective-permute-start(f32[1,32,1024]{2,1,0:T(8,128)S(1)} %get-tuple-element.21), channel_id=1, source_target_pairs={{0,1},{1,2},{2,3},{3,4},{4,5},{5,6},{6,7},{8,9},{9,10},{10,11},{11... | collective-permute-start | bytes 393224 | tf_op jit(solution)/shard_map/ppermute | solution.py:33
  11.1 2.5 %copy-start.1 = (bf16[3,1,16,32,1024]{4,3,2,1,0:T(8,128)(2,1)S(1)}, bf16[3,1,16,32,1024]{4,3,2,1,0:T(8,128)(2,1)}, u32[]{:S(2)}) copy-start(bf16[3,1,16,32,1024]{4,3,2,1,0:T(8,128)(2,1)} %param.9) | copy-start | bytes 9437188
  11.1 2.8 %copy-start.2 = (bf16[1,16,32,1024]{3,2,1,0:T(8,128)(2,1)S(1)}, bf16[1,16,32,1024]{3,2,1,0:T(8,128)(2,1)}, u32[]{:S(2)}) copy-start(bf16[1,16,32,1024]{3,2,1,0:T(8,128)(2,1)} %param.8) | copy-start | bytes 3145732
  19.4 6.7 %collective-permute-start.2 = (f32[1,32,1024]{2,1,0:T(8,128)S(1)}, f32[1,32,1024]{2,1,0:T(8,128)S(1)}, u32[]{:S(2)}, u32[]{:S(2)}) collective-permute-start(f32[1,32,1024]{2,1,0:T(8,128)S(1)} %get-tuple-element.20), channel_id=1, source_target_pairs={{1,0},{2,1},{3,2},{4,3},{5,4},{6,5},{7,6},{9,8},{10,9},{11,10},{12... | collective-permute-start | bytes 393224 | tf_op jit(solution)/shard_map/ppermute | solution.py:35
  21.8 5.5 %collective-permute-start.3 = (f32[1,32,1024]{2,1,0:T(8,128)S(1)}, f32[1,32,1024]{2,1,0:T(8,128)S(1)}, u32[]{:S(2)}, u32[]{:S(2)}) collective-permute-start(f32[1,32,1024]{2,1,0:T(8,128)S(1)} %get-tuple-element.19), channel_id=1, source_target_pairs={{0,1},{1,2},{2,3},{3,4},{4,5},{5,6},{6,7},{8,9},{9,10},{10,11},{11... | collective-permute-start | bytes 393224 | tf_op jit(solution)/shard_map/ppermute | solution.py:33
  33.4 7.0 %collective-permute-start.4 = (f32[1,32,1024]{2,1,0:T(8,128)S(1)}, f32[1,32,1024]{2,1,0:T(8,128)S(1)}, u32[]{:S(2)}, u32[]{:S(2)}) collective-permute-start(f32[1,32,1024]{2,1,0:T(8,128)S(1)} %get-tuple-element.18), channel_id=1, source_target_pairs={{1,0},{2,1},{3,2},{4,3},{5,4},{6,5},{7,6},{9,8},{10,9},{11,10},{12... | collective-permute-start | bytes 393224 | tf_op jit(solution)/shard_map/ppermute | solution.py:35
  35.3 6.3 %collective-permute-start.5 = (f32[1,32,1024]{2,1,0:T(8,128)S(1)}, f32[1,32,1024]{2,1,0:T(8,128)S(1)}, u32[]{:S(2)}, u32[]{:S(2)}) collective-permute-start(f32[1,32,1024]{2,1,0:T(8,128)S(1)} %get-tuple-element.17), channel_id=1, source_target_pairs={{0,1},{1,2},{2,3},{3,4},{4,5},{5,6},{6,7},{8,9},{9,10},{10,11},{11... | collective-permute-start | bytes 393224 | tf_op jit(solution)/shard_map/ppermute | solution.py:33
  47.7 7.0 %collective-permute-start.6 = (f32[1,32,1024]{2,1,0:T(8,128)S(1)}, f32[1,32,1024]{2,1,0:T(8,128)S(1)}, u32[]{:S(2)}, u32[]{:S(2)}) collective-permute-start(f32[1,32,1024]{2,1,0:T(8,128)S(1)} %get-tuple-element.16), channel_id=1, source_target_pairs={{1,0},{2,1},{3,2},{4,3},{5,4},{6,5},{7,6},{9,8},{10,9},{11,10},{12... | collective-permute-start | bytes 393224 | tf_op jit(solution)/shard_map/ppermute | solution.py:35
  49.6 6.3 %collective-permute-start.7 = (f32[1,32,1024]{2,1,0:T(8,128)S(1)}, f32[1,32,1024]{2,1,0:T(8,128)S(1)}, u32[]{:S(2)}, u32[]{:S(2)}) collective-permute-start(f32[1,32,1024]{2,1,0:T(8,128)S(1)} %get-tuple-element.15), channel_id=1, source_target_pairs={{0,1},{1,2},{2,3},{3,4},{4,5},{5,6},{6,7},{8,9},{9,10},{10,11},{11... | collective-permute-start | bytes 393224 | tf_op jit(solution)/shard_map/ppermute | solution.py:33
  56.6 12.2 %copy-start.5 = (f32[1,256,128]{2,1,0:T(8,128)S(1)}, f32[1,256,128]{2,1,0:T(8,128)}, u32[]{:S(2)}) copy-start(f32[1,256,128]{2,1,0:T(8,128)} %param.12) | copy-start | bytes 393220
  56.6 23.4 %copy-start.6 = (s32[1,256]{1,0:T(1,128)S(1)}, s32[1,256]{1,0:T(1,128)}, u32[]{:S(2)}) copy-start(s32[1,256]{1,0:T(1,128)} %param.11) | copy-start | bytes 3076
  62.0 58.2 %copy-start.4 = (f32[16,32,1024]{2,1,0:T(8,128)}, f32[16,32,1024]{2,1,0:T(8,128)S(1)}, u32[]{:S(2)}) copy-start(f32[16,32,1024]{2,1,0:T(8,128)S(1)} %fusion.11) | copy-start | bytes 6291460
  62.0 52.6 %copy-start.7 = (f32[1,256]{1,0:T(1,128)S(1)}, f32[1,256]{1,0:T(1,128)}, u32[]{:S(2)}) copy-start(f32[1,256]{1,0:T(1,128)} %param.10) | copy-start | bytes 3076
  62.5 7.3 %collective-permute-start.8 = (f32[1,256]{1,0:T(1,128)S(1)}, f32[1,256]{1,0:T(1,128)S(1)}, u32[]{:S(2)}, u32[]{:S(2)}) collective-permute-start(f32[1,256]{1,0:T(1,128)S(1)} %div.18), channel_id=1, source_target_pairs={{0,128},{8,136},{16,144},{24,152},{32,160},{40,168},{48,176},{56,1... | collective-permute-start | bytes 3080 | tf_op jit(solution)/shard_map/ppermute | solution.py:45
  69.8 8.6 %collective-permute-start.9 = (f32[1,256]{1,0:T(1,128)S(1)}, f32[1,256]{1,0:T(1,128)S(1)}, u32[]{:S(2)}, u32[]{:S(2)}) collective-permute-start(f32[1,256]{1,0:T(1,128)S(1)} %collective-permute-done.8), channel_id=1, source_target_pairs={{0,1},{1,2},{2,3},{3,4},{4,5},{5,6},{6,7},{7,0},{8,9},{9,10},{10,1... | collective-permute-start | bytes 3080 | tf_op jit(solution)/shard_map/ppermute | solution.py:18
  74.0 12.0 %all-to-all-start = ((f32[8,16,128]{2,1,0:T(8,128)}), f32[8,16,128]{2,1,0:T(8,128)S(1)}, u32[]{:S(2)}, u32[]{:S(2)}) async-start(f32[8,16,128]{2,1,0:T(8,128)} %fusion.37), calls=%async_computation | async-start | bytes 131072 | tf_op jit(solution)/shard_map/all_to_all | solution.py:57
  78.4 2.4 %collective-permute-start.10 = (f32[1,256]{1,0:T(1,128)S(1)}, f32[1,256]{1,0:T(1,128)S(1)}, u32[]{:S(2)}, u32[]{:S(2)}) collective-permute-start(f32[1,256]{1,0:T(1,128)S(1)} %collective-permute-done.9), channel_id=1, source_target_pairs={{0,1},{1,2},{2,3},{3,4},{4,5},{5,6},{6,7},{7,0},{8,9},{9,10},{10,1... | collective-permute-start | bytes 3080 | tf_op jit(solution)/shard_map/ppermute | solution.py:18
  80.0 3.3 %collective-permute-start.13 = (f32[1,256]{1,0:T(1,128)S(1)}, f32[1,256]{1,0:T(1,128)S(1)}, u32[]{:S(2)}, u32[]{:S(2)}) collective-permute-start(f32[1,256]{1,0:T(1,128)S(1)} %collective-permute-done.8), channel_id=1, source_target_pairs={{0,7},{1,0},{2,1},{3,2},{4,3},{5,4},{6,5},{7,6},{8,15},{9,8},{10,9... | collective-permute-start | bytes 3080 | tf_op jit(solution)/shard_map/ppermute | solution.py:20
  80.7 3.0 %collective-permute-start.11 = (f32[1,256]{1,0:T(1,128)S(1)}, f32[1,256]{1,0:T(1,128)S(1)}, u32[]{:S(2)}, u32[]{:S(2)}) collective-permute-start(f32[1,256]{1,0:T(1,128)S(1)} %collective-permute-done.10), channel_id=1, source_target_pairs={{0,1},{1,2},{2,3},{3,4},{4,5},{5,6},{6,7},{7,0},{8,9},{9,10},{10,1... | collective-permute-start | bytes 3080 | tf_op jit(solution)/shard_map/ppermute | solution.py:18
  83.3 13.4 %collective-permute-start.14 = (f32[1,256]{1,0:T(1,128)S(1)}, f32[1,256]{1,0:T(1,128)S(1)}, u32[]{:S(2)}, u32[]{:S(2)}) collective-permute-start(f32[1,256]{1,0:T(1,128)S(1)} %collective-permute-done.13), channel_id=1, source_target_pairs={{0,7},{1,0},{2,1},{3,2},{4,3},{5,4},{6,5},{7,6},{8,15},{9,8},{10,9... | collective-permute-start | bytes 3080 | tf_op jit(solution)/shard_map/ppermute | solution.py:20
  83.7 14.5 %collective-permute-start.12 = (f32[1,256]{1,0:T(1,128)S(1)}, f32[1,256]{1,0:T(1,128)S(1)}, u32[]{:S(2)}, u32[]{:S(2)}) collective-permute-start(f32[1,256]{1,0:T(1,128)S(1)} %collective-permute-done.11), channel_id=1, source_target_pairs={{0,1},{1,2},{2,3},{3,4},{4,5},{5,6},{6,7},{7,0},{8,9},{9,10},{10,1... | collective-permute-start | bytes 3080 | tf_op jit(solution)/shard_map/ppermute | solution.py:18
  86.7 20.5 %all-to-all-start.1 = ((f32[32,16,128]{2,1,0:T(8,128)}), f32[32,16,128]{2,1,0:T(8,128)S(1)}, u32[]{:S(2)}, u32[]{:S(2)}) async-start(f32[32,16,128]{2,1,0:T(8,128)} %broadcast_in_dim.51), calls=%async_computation.1 | async-start | bytes 524288 | tf_op jit(solution)/shard_map/all_to_all | solution.py:51
  96.7 3.0 %collective-permute-start.15 = (f32[1,256]{1,0:T(1,128)S(1)}, f32[1,256]{1,0:T(1,128)S(1)}, u32[]{:S(2)}, u32[]{:S(2)}) collective-permute-start(f32[1,256]{1,0:T(1,128)S(1)} %collective-permute-done.14), channel_id=1, source_target_pairs={{0,7},{1,0},{2,1},{3,2},{4,3},{5,4},{6,5},{7,6},{8,15},{9,8},{10,9... | collective-permute-start | bytes 3080 | tf_op jit(solution)/shard_map/ppermute | solution.py:20
  108.0 11.5 %all-to-all-start.2 = ((f32[8,16,128]{2,1,0:T(8,128)}), f32[8,16,128]{2,1,0:T(8,128)S(1)}, u32[]{:S(2)}, u32[]{:S(2)}) async-start(f32[8,16,128]{2,1,0:T(8,128)} %broadcast_in_dim.52), calls=%async_computation.2 | async-start | bytes 131072 | tf_op jit(solution)/shard_map/all_to_all | solution.py:60
  120.2 29.8 %all-to-all-start.3 = ((f32[256,1,128]{2,1,0:T(1,128)}), f32[256,1,128]{2,1,0:T(1,128)S(1)}, u32[]{:S(2)}, u32[]{:S(2)}) async-start(f32[256,1,128]{2,1,0:T(1,128)} %broadcast_in_dim.54), calls=%async_computation.3 | async-start | bytes 262144 | tf_op jit(solution)/shard_map/all_to_all | solution.py:51
